TPU v7x, 256 devices: a whole 4x4x8 slice. The times are simulated.
256 devices in a mesh: expert: 64 (over y_hi, x, z), half: 2 (over y_lo), dp: 2 (over core).
Axes of the slice: x: 4, y: 4 (y_hi: 2, y_lo: 2; y = y_hi * 2 + y_lo), z: 8, core: 2. Of those that a mesh axis runs over, the one named last changes fastest.
Arguments:
- tokens: bfloat16 [16384, 4096], P(('expert', 'dp'), 'half'), may hold values from -6 to 6
- cotangent: bfloat16 [16384, 4096], P(('expert', 'dp'), 'half'), may hold values from -12 to 12
- expert_ids: int32 [16384, 8], P(('expert', 'dp')), may hold values from 0 to 63, as said below
- slot_ids: int32 [16384, 8], P(('expert', 'dp')), may hold values from 0 to 17, as said below
- gate_weights: float32 [16384, 8], P(('expert', 'dp')), may hold values from 0.03 to 0.4
- latent_down: bfloat16 [4096, 1024], P('half', 'dp'), may hold values from -0.09375 to 0.09375
- latent_up: bfloat16 [1024, 4096], P('dp', 'half'), may hold values from -0.1875 to 0.1875
- expert_gate: bfloat16 [64, 1024, 1536], P('expert', 'dp', 'half'), may hold values from -0.1875 to 0.1875
- expert_linear: bfloat16 [64, 1024, 1536], P('expert', 'dp', 'half'), may hold values from -0.1875 to 0.1875
- expert_out: bfloat16 [64, 1536, 1024], P('expert', 'half', 'dp'), may hold values from -0.15625 to 0.15625
Outputs:
- token_grad: bfloat16 [16384, 4096], P(('expert', 'dp'), 'half')
- gate_grad: bfloat16 [64, 1024, 1536], P('expert', 'dp', 'half')
- linear_grad: bfloat16 [64, 1024, 1536], P('expert', 'dp', 'half')
- out_grad: bfloat16 [64, 1536, 1024], P('expert', 'half', 'dp')
Inputs may be any that keep to these rules, and one draw needn't show every extreme that they name: `expert_ids`: each row names 8 different experts. In each aligned block of 128 rows (the rows of one device) no expert is named by more than 18 rows, and one expert is named by exactly 18 rows in every block. `slot_ids`: within one aligned block of 128 rows, the entries that name the same expert have different slots.
All inputs are finite; a program needn't handle non-finite values.
Results may differ from a plain program's by a relative error of at most 0.013.
Values may be sent and summed in bfloat16 or wider, within the bound.
A program may use at most 128 MiB of HBM per device.

v0:
```python
import jax
import jax.numpy as jnp
from jax import lax
from jax.sharding import PartitionSpec as P


def on_device(
    tokens,
    cotangent,
    expert_ids,
    slot_ids,
    gate_weights,
    latent_down,
    latent_up,
    expert_gate,
    expert_linear,
    expert_out,
):
    row_count = tokens.shape[0]
    pick_count = expert_ids.shape[1]
    local_count = expert_gate.shape[0]
    group_count = lax.axis_size("expert")
    expert_count = group_count * local_count
    capacity = min(
        row_count, 2 * ((9 * row_count * pick_count + 16 * expert_count - 1) // (16 * expert_count))
    )
    down_full, up_full, gate_full, linear_full, output_full = (
        lax.all_gather(latent_down, "dp", axis=1, tiled=True),
        lax.all_gather(latent_up, "dp", axis=0, tiled=True),
        lax.all_gather(expert_gate, "dp", axis=1, tiled=True),
        lax.all_gather(expert_linear, "dp", axis=1, tiled=True),
        lax.all_gather(expert_out, "dp", axis=2, tiled=True),
    )
    latent_part = jnp.dot(tokens, down_full, preferred_element_type=jnp.float32)
    back_part = lax.dot_general(
        cotangent, up_full, (((1,), (1,)), ((), ())), preferred_element_type=jnp.float32
    )
    latent_sum, back_latent = lax.psum((latent_part, back_part), "half")
    latent = latent_sum.astype(jnp.bfloat16)
    width = latent.shape[1]
    flat_slot = (expert_ids * capacity + slot_ids).reshape(-1)
    slot_table = lax.broadcasted_iota(
        jnp.int32, (expert_count * capacity, row_count * pick_count), 0
    )
    matches = flat_slot[None, :] == slot_table
    choice_index = lax.broadcasted_iota(jnp.int32, matches.shape, 1)
    source = jnp.sum(jnp.where(matches, choice_index, 0), axis=1)
    filled = jnp.any(matches, axis=1)
    token_of = source // pick_count
    gate_of = gate_weights.reshape(-1)[source]
    send_latent = jnp.where(filled[:, None], latent[token_of], jnp.zeros((), jnp.bfloat16))
    send_back = jnp.where(filled[:, None], gate_of[:, None] * back_latent[token_of], 0.0).astype(
        jnp.bfloat16
    )
    send_latent = send_latent.reshape(group_count, local_count, capacity, width)
    send_back = send_back.reshape(group_count, local_count, capacity, width)
    rows_latent, rows_back = (
        lax.all_to_all(send_latent, "expert", split_axis=0, concat_axis=0, tiled=True),
        lax.all_to_all(send_back, "expert", split_axis=0, concat_axis=0, tiled=True),
    )
    pre_gate = jnp.einsum(
        "neci,eih->nech", rows_latent, gate_full, preferred_element_type=jnp.float32
    )
    pre_linear = jnp.einsum(
        "neci,eih->nech", rows_latent, linear_full, preferred_element_type=jnp.float32
    )
    grad_hidden = jnp.einsum(
        "necj,ehj->nech", rows_back, output_full, preferred_element_type=jnp.float32
    )
    logistic = jax.nn.sigmoid(pre_gate)
    hidden = (pre_gate * logistic * pre_linear).astype(jnp.bfloat16)
    gate_delta = (grad_hidden * pre_linear * logistic * (1.0 + pre_gate * (1.0 - logistic))).astype(
        jnp.bfloat16
    )
    linear_delta = (grad_hidden * pre_gate * logistic).astype(jnp.bfloat16)
    gate_part = jnp.einsum(
        "neci,nech->eih", rows_latent, gate_delta, preferred_element_type=jnp.float32
    )
    linear_part = jnp.einsum(
        "neci,nech->eih", rows_latent, linear_delta, preferred_element_type=jnp.float32
    )
    out_part = jnp.einsum("nech,necj->ehj", hidden, rows_back, preferred_element_type=jnp.float32)
    gate_share, linear_share, out_share = (
        lax.psum_scatter(
            gate_part.astype(jnp.bfloat16), "dp", scatter_dimension=1, tiled=True
        ).astype(jnp.float32),
        lax.psum_scatter(
            linear_part.astype(jnp.bfloat16), "dp", scatter_dimension=1, tiled=True
        ).astype(jnp.float32),
        lax.psum_scatter(
            out_part.astype(jnp.bfloat16), "dp", scatter_dimension=2, tiled=True
        ).astype(jnp.float32),
    )
    row_part = jnp.einsum(
        "nech,eih->neci", gate_delta, gate_full, preferred_element_type=jnp.float32
    )
    row_part = row_part + jnp.einsum(
        "nech,eih->neci", linear_delta, linear_full, preferred_element_type=jnp.float32
    )
    row_whole = lax.psum(row_part, "half").astype(jnp.bfloat16)
    returned = lax.all_to_all(row_whole, "expert", split_axis=0, concat_axis=0, tiled=True)
    position = expert_ids * capacity + slot_ids
    gathered = returned.reshape(expert_count * capacity, width)[position]
    latent_grad = jnp.sum(gathered.astype(jnp.float32), axis=1)
    token_grad = lax.dot_general(
        latent_grad.astype(jnp.bfloat16),
        down_full,
        (((1,), (1,)), ((), ())),
        preferred_element_type=jnp.float32,
    )
    return (
        token_grad.astype(jnp.bfloat16),
        gate_share.astype(jnp.bfloat16),
        linear_share.astype(jnp.bfloat16),
        out_share.astype(jnp.bfloat16),
    )


def solution(mesh):
    in_specs = (
        P(("expert", "dp"), "half"),
        P(("expert", "dp"), "half"),
        P(("expert", "dp"), None),
        P(("expert", "dp"), None),
        P(("expert", "dp"), None),
        P("half", "dp"),
        P("dp", "half"),
        P("expert", "dp", "half"),
        P("expert", "dp", "half"),
        P("expert", "half", "dp"),
    )
    out_specs = (
        P(("expert", "dp"), "half"),
        P("expert", "dp", "half"),
        P("expert", "dp", "half"),
        P("expert", "half", "dp"),
    )
    return jax.shard_map(
        on_device, mesh=mesh, in_specs=in_specs, out_specs=out_specs, check_vma=False
    )
```

profile of v0, /device:TPU:64, one launch (start us, length us, event | category | flops | bytes accessed | tf_op | source)
XLA Modules:
  0.0 496.2 jit_solution(3944161558312490674)
XLA Ops:
  7.2 0.7 all-gather.10.cloned.1.call-update
  8.0 0.7 all-gather.6.cloned.1.call-update
  8.7 0.1 copy.38
  8.9 0.6 fusion.2
  9.5 0.6 select_reduce_fusion
  10.1 0.1 broadcast_in_dim.37
  10.4 20.7 %all-gather.10.cloned.1.call-done = bf16[2048,1024]{1,0:T(8,128)(2,1)} async-done(((bf16[2048,512]{1,0:T(8,128)(2,1)}), bf16[2048,1024]{1,0:T(8,128)(2,1)}) %all-gather.10.cloned.1.call-update) | async-done | bytes 4194320 | tf_op jit(solution)/shard_map/all_gather | solution.py:28
  31.1 2.9 fusion.74
  34.0 18.1 %all-reduce.5 = bf16[128,1024]{1,0:T(8,128)(2,1)S(1)} all-reduce(f32[128,1024]{1,0:T(8,128)S(1)} %fusion.74), channel_id=1, replica_groups=mesh['expert'=64,'half'=2,'dp'=2] {'half'}, use_global_device_ids=true, to_apply=%region_3.4 | all-reduce | flops 131072 | bytes 786432 | tf_op jit(solution)/shard_map/psum | solution.py:38
  52.1 4.4 gather_fusion.2
  56.5 2.4 gather.20
  59.0 4.7 copy_select_fusion
  63.6 3.1 copy.46
  66.7 12.8 %all-to-all-start.1 = ((bf16[64,1,18,1024]{3,2,1,0:T(8,128)(2,1)}), bf16[64,1,18,1024]{3,2,1,0:T(8,128)(2,1)}, u32[]{:S(2)}, u32[]{:S(2)}) async-start(bf16[64,1,18,1024]{3,2,1,0:T(8,128)(2,1)} %copy.46), calls=%async_computation.1 | async-start | bytes 6291456 | tf_op jit(solution)/shard_map/all_to_all | solution.py:58
  79.5 0.2 all-reduce.4.cloned.1.call-start
  79.8 4.5 fusion.73
  84.5 4.6 gather_fusion
  89.1 0.1 mul.46
  89.3 49.1 %all-reduce.4.cloned.1.call-done = f32[128,1024]{1,0:T(8,128)} async-done(((f32[128,1024]{1,0:T(8,128)}), f32[128,1024]{1,0:T(8,128)}) %all-reduce.4.cloned.1.call-update) | async-done | bytes 524304 | tf_op jit(solution)/shard_map/psum | solution.py:38
  138.4 7.6 %gather_fusion.1 = f32[1152,1024]{1,0:T(8,128)} fusion(f32[128,1024]{1,0:T(8,128)} %all-reduce.4.cloned.1.call-done, s32[2048]{0:T(1024)S(1)} %pad_clamp_fusion), kind=kCustom, calls=%fused_computation.1 | custom fusion | bytes 9441792 | tf_op jit(solution)/shard_map/gather | solution.py:52
  146.0 5.6 %gather.18 = f32[64,1,18,1024]{3,2,0,1:T(8,128)} reshape(f32[1152,1024]{1,0:T(8,128)} %gather_fusion.1) | data formatting | bytes 9437184 | tf_op jit(solution)/shard_map/gather | solution.py:52
  151.6 5.6 %fusion.1 = bf16[64,1,18,1024]{3,0,2,1:T(8,128)(2,1)S(1)} fusion(f32[64,1,18,1024]{3,2,0,1:T(8,128)} %gather.18, f32[64,18]{0,1:T(8,128)S(1)} %copy.41, pred[64,18]{0,1:T(8,128)(4,1)S(1)} %copy.39), kind=kLoop, calls=%fused_computation.6 | loop fusion | flops 3538944 | bytes 7083648 | tf_op jit(solution)/shard_map/convert_element_type | solution.py:52
  157.2 3.0 copy.43
  160.3 11.9 %all-to-all-start = ((bf16[64,1,18,1024]{3,2,1,0:T(8,128)(2,1)}), bf16[64,1,18,1024]{3,2,1,0:T(8,128)(2,1)}, u32[]{:S(2)}, u32[]{:S(2)}) async-start(bf16[64,1,18,1024]{3,2,1,0:T(8,128)(2,1)} %copy.43), calls=%async_computation | async-start | bytes 6291456 | tf_op jit(solution)/shard_map/all_to_all | solution.py:59
  172.3 0.5 all-gather.14.cloned.1.call-update
  172.8 0.5 all-gather.12.cloned.1.call-update
  173.4 0.5 all-gather.8.cloned.1.call-update
  174.0 0.3 reduce-scatter.8.cloned.1.call-start
  174.2 16.9 %all-gather.14.cloned.1.call-done = bf16[1,1024,768]{2,1,0:T(8,128)(2,1)} async-done(((bf16[1,512,768]{2,1,0:T(8,128)(2,1)}), bf16[1,1024,768]{2,1,0:T(8,128)(2,1)}) %all-gather.14.cloned.1.call-update) | async-done | bytes 1572880 | tf_op jit(solution)/shard_map/all_gather | solution.py:30
  191.1 8.2 %fusion.17 = f32[64,18,768]{2,0,1:T(8,128)} fusion(bf16[1,1024,768]{2,1,0:T(8,128)(2,1)} %all-gather.14.cloned.1.call-done, bf16[64,1,18,1024]{3,2,1,0:T(8,128)(2,1)} %all-to-all-done.1), kind=kOutput, calls=%fused_computation.35 | convolution fusion | flops 1811939328 | bytes 7471104 | tf_op jit(solution)/shard_map/neci,eih->nech/dot_general | solution.py:61
  199.3 10.1 %all-gather.12.cloned.1.call-done = bf16[1,1024,768]{2,1,0:T(8,128)(2,1)} async-done(((bf16[1,512,768]{2,1,0:T(8,128)(2,1)}), bf16[1,1024,768]{2,1,0:T(8,128)(2,1)}) %all-gather.12.cloned.1.call-update) | async-done | bytes 1572880 | tf_op jit(solution)/shard_map/all_gather | solution.py:31
  209.4 8.2 %fusion.19 = f32[64,18,768]{2,0,1:T(8,128)} fusion(bf16[1,1024,768]{2,1,0:T(8,128)(2,1)} %all-gather.12.cloned.1.call-done, bf16[64,1,18,1024]{3,2,1,0:T(8,128)(2,1)} %all-to-all-done.1), kind=kOutput, calls=%fused_computation.37 | convolution fusion | flops 1811939328 | bytes 7471104 | tf_op jit(solution)/shard_map/neci,eih->nech/dot_general | solution.py:64
  217.6 28.6 %all-to-all-done = bf16[64,1,18,1024]{3,2,1,0:T(8,128)(2,1)} async-done(((bf16[64,1,18,1024]{3,2,1,0:T(8,128)(2,1)}), bf16[64,1,18,1024]{3,2,1,0:T(8,128)(2,1)}, u32[]{:S(2)}, u32[]{:S(2)}) %all-to-all-start) | async-done | bytes 2359328 | tf_op jit(solution)/shard_map/all_to_all | solution.py:59
  246.2 9.5 %fusion.61 = bf16[1,768,1024]{2,1,0:T(8,128)(2,1)} fusion(bf16[64,1,18,1024]{3,2,1,0:T(8,128)(2,1)} %all-to-all-done, f32[64,18,768]{2,0,1:T(8,128)} %fusion.19, f32[64,18,768]{2,0,1:T(8,128)} %fusion.17), kind=kOutput, calls=%fused_computation.60 | convolution fusion | flops 1818034176 | bytes 11010048 | tf_op jit(solution)/shard_map/nech,necj->ehj/dot_general | solution.py:82
  255.7 0.4 reduce-scatter.4.cloned.1.call-start
  256.2 9.3 %fusion.8 = (bf16[64,1,18,768]{3,0,2,1:T(8,128)(2,1)S(1)}, bf16[64,1,18,768]{3,0,2,1:T(8,128)(2,1)S(1)}) fusion(f32[64,18,768]{2,0,1:T(8,128)} %fusion.17, f32[64,18,768]{2,0,1:T(8,128)} %fusion.19, bf16[1,768,1024]{2,1,0:T(8,128)(2,1)} %all-gather.8.cloned.1.call-done, bf16[64,1,18,1024]{3,2,1,0:T(8,128)(2,1)} %all-to-all-done), kind=kOutput, calls=%fused_computation.19 | convolution fusion | flops 1823440896 | bytes 14548992 | tf_op jit(solution)/shard_map/necj,ehj->nech/dot_general | solution.py:67
  265.6 2.1 fusion.29
  267.6 4.2 add_bitcast_fusion
  271.8 6.1 %fusion.51 = bf16[1,1024,768]{2,1,0:T(8,128)(2,1)} fusion(bf16[64,1,18,768]{3,0,2,1:T(8,128)(2,1)S(1)} %get-tuple-element.9, bf16[64,1,18,1024]{3,2,1,0:T(8,128)(2,1)} %all-to-all-done.1), kind=kOutput, calls=%fused_computation.58 | convolution fusion | flops 1812725760 | bytes 5701632 | tf_op jit(solution)/shard_map/neci,nech->eih/dot_general | solution.py:76
  278.0 110.2 %all-reduce.6 = bf16[64,1,18,1024]{3,0,2,1:T(8,128)(2,1)S(1)} all-reduce(f32[64,1,18,1024]{3,0,2,1:T(8,128)} %add_bitcast_fusion), channel_id=1, replica_groups=mesh['expert'=64,'half'=2,'dp'=2] {'half'}, use_global_device_ids=true, to_apply=%region_4.5 | all-reduce | flops 1179648 | bytes 7077888 | tf_op jit(solution)/shard_map/psum | solution.py:100
  388.1 3.0 copy.48
  391.1 9.8 %all-to-all-start.2 = ((bf16[64,1,18,1024]{3,2,1,0:T(8,128)(2,1)}), bf16[64,1,18,1024]{3,2,1,0:T(8,128)(2,1)}, u32[]{:S(2)}, u32[]{:S(2)}) async-start(bf16[64,1,18,1024]{3,2,1,0:T(8,128)(2,1)} %copy.48), calls=%async_computation.2 | async-start | bytes 6291456 | tf_op jit(solution)/shard_map/all_to_all | solution.py:101
  401.0 6.0 %fusion.56 = bf16[1,1024,768]{2,1,0:T(8,128)(2,1)} fusion(bf16[64,1,18,768]{3,0,2,1:T(8,128)(2,1)S(1)} %copy-done.9, bf16[64,1,18,1024]{3,2,1,0:T(8,128)(2,1)} %all-to-all-done.1), kind=kOutput, calls=%fused_computation.59 | convolution fusion | flops 1812725760 | bytes 5701632 | tf_op jit(solution)/shard_map/neci,nech->eih/dot_general | solution.py:79
  407.2 66.4 %all-to-all-done.2 = bf16[64,1,18,1024]{3,2,1,0:T(8,128)(2,1)} async-done(((bf16[64,1,18,1024]{3,2,1,0:T(8,128)(2,1)}), bf16[64,1,18,1024]{3,2,1,0:T(8,128)(2,1)}, u32[]{:S(2)}, u32[]{:S(2)}) %all-to-all-start.2) | async-done | bytes 2359328 | tf_op jit(solution)/shard_map/all_to_all | solution.py:101
  473.6 2.9 reshape.185
  476.5 5.4 %gather_fusion.3 = bf16[1024,1024]{1,0:T(8,128)(2,1)} fusion(bf16[1152,1024]{1,0:T(8,128)(2,1)S(1)} %reshape.185, s32[1024]{0:T(1024)S(1)} %broadcast_clamp_fusion), kind=kCustom, calls=%fused_computation.3 | custom fusion | bytes 4198400 | tf_op jit(solution)/shard_map/gather | solution.py:103
  481.9 3.0 bitcast_reduce_fusion
  484.9 4.5 convolution_convert_fusion
  (48 shorter events, 1.1 us)
Async XLA Ops:
  7.2 24.0 %copy-start = (bf16[128,2048]{1,0:T(8,128)(2,1)S(1)}, bf16[128,2048]{1,0:T(8,128)(2,1)}, u32[]{:S(2)}) copy-start(bf16[128,2048]{1,0:T(8,128)(2,1)} %param.10) | copy-start | bytes 1572868
  7.2 1.5 copy-start.4
  7.2 1.5 copy-start.5
  7.2 23.9 %all-gather.10.cloned.1.call-start = ((), (), s32[]{:S(2)}) async-start(), calls=%async_computation.9 | async-start | bytes 6291456 | tf_op jit(solution)/shard_map/all_gather | solution.py:28
  7.9 71.8 %all-gather.6.cloned.1.call-start = ((), (), s32[]{:S(2)}) async-start(), calls=%async_computation.6 | async-start | bytes 6291456 | tf_op jit(solution)/shard_map/all_gather | solution.py:29
  66.7 13.1 %copy-start.2 = (bf16[128,2048]{1,0:T(8,128)(2,1)S(1)}, bf16[128,2048]{1,0:T(8,128)(2,1)}, u32[]{:S(2)}) copy-start(bf16[128,2048]{1,0:T(8,128)(2,1)} %param.11) | copy-start | bytes 1572868
  66.7 93.6 %all-to-all-start.1 = ((bf16[64,1,18,1024]{3,2,1,0:T(8,128)(2,1)}), bf16[64,1,18,1024]{3,2,1,0:T(8,128)(2,1)}, u32[]{:S(2)}, u32[]{:S(2)}) async-start(bf16[64,1,18,1024]{3,2,1,0:T(8,128)(2,1)} %copy.46), calls=%async_computation.1 | async-start | bytes 6291456 | tf_op jit(solution)/shard_map/all_to_all | solution.py:58
  79.5 4.8 copy-start.3
  79.5 58.9 %all-reduce.4.cloned.1.call-start = ((), (), s32[]{:S(2)}) async-start(), calls=%async_computation.7 | async-start | bytes 1048576 | tf_op jit(solution)/shard_map/psum | solution.py:38
  160.3 85.9 %all-to-all-start = ((bf16[64,1,18,1024]{3,2,1,0:T(8,128)(2,1)}), bf16[64,1,18,1024]{3,2,1,0:T(8,128)(2,1)}, u32[]{:S(2)}, u32[]{:S(2)}) async-start(bf16[64,1,18,1024]{3,2,1,0:T(8,128)(2,1)} %copy.43), calls=%async_computation | async-start | bytes 6291456 | tf_op jit(solution)/shard_map/all_to_all | solution.py:59
  172.2 18.9 %all-gather.14.cloned.1.call-start = ((), (), s32[]{:S(2)}) async-start(), calls=%async_computation.11 | async-start | bytes 2359296 | tf_op jit(solution)/shard_map/all_gather | solution.py:30
  172.8 36.6 %all-gather.12.cloned.1.call-start = ((), (), s32[]{:S(2)}) async-start(), calls=%async_computation.10 | async-start | bytes 2359296 | tf_op jit(solution)/shard_map/all_gather | solution.py:31
  173.4 82.8 %all-gather.8.cloned.1.call-start = ((), (), s32[]{:S(2)}) async-start(), calls=%async_computation.8 | async-start | bytes 2359296 | tf_op jit(solution)/shard_map/all_gather | solution.py:32
  174.0 315.5 %reduce-scatter.8.cloned.1.call-start = ((), (), s32[]{:S(2)}) async-start(), calls=%async_computation.14 | async-start | bytes 2359296 | tf_op jit(solution)/shard_map/reduce_scatter | solution.py:90
  255.7 9.8 %copy-start.6 = (bf16[1,1024,768]{2,1,0:T(8,128)(2,1)S(1)}, bf16[1,1024,768]{2,1,0:T(8,128)(2,1)}, u32[]{:S(2)}) copy-start(bf16[1,1024,768]{2,1,0:T(8,128)(2,1)} %all-gather.14.cloned.1.call-done) | copy-start | bytes 4718596
  255.7 233.7 %reduce-scatter.4.cloned.1.call-start = ((), (), s32[]{:S(2)}) async-start(), calls=%async_computation.12 | async-start | bytes 2359296 | tf_op jit(solution)/shard_map/reduce_scatter | solution.py:84
  265.5 2.1 copy-start.8
  265.5 2.1 copy-start.7
  391.1 9.8 %copy-start.9 = (bf16[64,1,18,768]{3,0,2,1:T(8,128)(2,1)S(1)}, bf16[64,1,18,768]{3,0,2,1:T(8,128)(2,1)}, u32[]{:S(2)}) copy-start(bf16[64,1,18,768]{3,0,2,1:T(8,128)(2,1)} %copy-done.8) | copy-start | bytes 5308420
  391.1 82.5 %all-to-all-start.2 = ((bf16[64,1,18,1024]{3,2,1,0:T(8,128)(2,1)}), bf16[64,1,18,1024]{3,2,1,0:T(8,128)(2,1)}, u32[]{:S(2)}, u32[]{:S(2)}) async-start(bf16[64,1,18,1024]{3,2,1,0:T(8,128)(2,1)} %copy.48), calls=%async_computation.2 | async-start | bytes 6291456 | tf_op jit(solution)/shard_map/all_to_all | solution.py:101
  400.9 88.6 %reduce-scatter.6.cloned.1.call-start = ((), (), s32[]{:S(2)}) async-start(), calls=%async_computation.13 | async-start | bytes 2359296 | tf_op jit(solution)/shard_map/reduce_scatter | solution.py:87
  476.5 12.9 %copy-start.1 = (bf16[128,2048]{1,0:T(8,128)(2,1)S(1)}, bf16[128,2048]{1,0:T(8,128)(2,1)}, u32[]{:S(2)}) copy-start(bf16[128,2048]{1,0:T(8,128)(2,1)} %param.10) | copy-start | bytes 1572868
Sparse Core Ops, SparseCore 0:
  9.8 21.2 all-gather.9
  32.9 20.2 all-gather.5
  84.4 53.9 all-reduce.3
  174.7 16.4 all-gather.13
  192.9 16.4 all-gather.11
  211.2 16.4 all-gather.7
  255.8 10.3 reduce-scatter.7
  278.1 10.3 reduce-scatter.3
  407.1 15.7 reduce-scatter.5
where the time goes:
time: 505 us; the launch traced here: 496 us
  waiting for transfers between devices  195 us (39%)
  blocking collectives  128 us (25%)
  matrix products  65.5 us (13%)
  local copies, waits for them, and re-layouts  43.1 us (9%)
  starting transfers between devices  35.6 us (7%)
  other arithmetic  14.6 us (3%)
  between operations  14.3 us (3%)
    psum x1, blocking collectives, on_device(): row_whole = lax.psum(row_part, 'half').astype(jnp.bfloat16)  110 us
    all_to_all x1, waiting for transfers between devices, on_device(): lax.all_to_all(row_whole, 'expert', split_axis=0, concat_axis=0, tiled=True)  66.4 us
    psum x1, waiting for transfers between devices, on_device(): latent_sum, back_latent = lax.psum((latent_part, back_part), 'half')  49.1 us
    all_to_all x1, waiting for transfers between devices, on_device(): lax.all_to_all(send_back, 'expert', split_axis=0, concat_axis=0, tiled=True)  28.6 us
    all_gather x1, waiting for transfers between devices, on_device(): lax.all_gather(latent_down, 'dp', axis=1, tiled=True)  20.7 us
    psum x1, blocking collectives, on_device(): latent_sum, back_latent = lax.psum((latent_part, back_part), 'half')  18.1 us
    all_gather x1, waiting for transfers between devices, on_device(): lax.all_gather(expert_gate, 'dp', axis=1, tiled=True)  16.9 us
    gather x2, local copies, waits for them, and re-layouts, on_device(): back_latent[token_of]  13.2 us
  transfers between devices with their start and end apart: 12, of which 6 were waited for; matrix products, arithmetic and copies ran while one was open for 25% of the time, Pallas kernels for 0%

commit v1 on v0

--- a/solution.py
+++ b/solution.py
@@ -1,7 +1,46 @@
+import functools
+
 import jax
 import jax.numpy as jnp
 from jax import lax
+from jax.experimental import pallas as pl
+from jax.experimental.pallas import tpu as pltpu
 from jax.sharding import PartitionSpec as P
+
+MESH = pl.DeviceIdType.MESH
+
+
+def _pair_sum_kernel(x_ref, o_ref, buf, send_sem, recv_sem):
+    other = 1 - lax.axis_index("half")
+    barrier = pltpu.get_barrier_semaphore()
+    pl.semaphore_signal(barrier, inc=1, device_id={"half": other}, device_id_type=MESH)
+    pl.semaphore_wait(barrier, 1)
+    copy = pltpu.make_async_remote_copy(
+        src_ref=x_ref,
+        dst_ref=buf,
+        send_sem=send_sem,
+        recv_sem=recv_sem,
+        device_id={"half": other},
+        device_id_type=MESH,
+    )
+    copy.start()
+    copy.wait()
+    o_ref[...] = x_ref[...] + buf[...]
+
+
+def pair_sum(x, collective_id):
+    return pl.pallas_call(
+        _pair_sum_kernel,
+        out_shape=jax.ShapeDtypeStruct(x.shape, x.dtype),
+        in_specs=[pl.BlockSpec(memory_space=pltpu.VMEM)],
+        out_specs=pl.BlockSpec(memory_space=pltpu.VMEM),
+        scratch_shapes=[
+            pltpu.VMEM(x.shape, x.dtype),
+            pltpu.SemaphoreType.DMA(()),
+            pltpu.SemaphoreType.DMA(()),
+        ],
+        compiler_params=pltpu.CompilerParams(collective_id=collective_id, has_side_effects=True),
+    )(x)
 
 
 def on_device(
@@ -35,9 +74,10 @@
     back_part = lax.dot_general(
         cotangent, up_full, (((1,), (1,)), ((), ())), preferred_element_type=jnp.float32
     )
-    latent_sum, back_latent = lax.psum((latent_part, back_part), "half")
-    latent = latent_sum.astype(jnp.bfloat16)
-    width = latent.shape[1]
+    width = latent_part.shape[1]
+    both = pair_sum(jnp.concatenate([latent_part, back_part], axis=1), 1)
+    latent = both[:, :width].astype(jnp.bfloat16)
+    back_latent = both[:, width:]
     flat_slot = (expert_ids * capacity + slot_ids).reshape(-1)
     slot_table = lax.broadcasted_iota(
         jnp.int32, (expert_count * capacity, row_count * pick_count), 0
@@ -52,12 +92,11 @@
     send_back = jnp.where(filled[:, None], gate_of[:, None] * back_latent[token_of], 0.0).astype(
         jnp.bfloat16
     )
-    send_latent = send_latent.reshape(group_count, local_count, capacity, width)
-    send_back = send_back.reshape(group_count, local_count, capacity, width)
-    rows_latent, rows_back = (
-        lax.all_to_all(send_latent, "expert", split_axis=0, concat_axis=0, tiled=True),
-        lax.all_to_all(send_back, "expert", split_axis=0, concat_axis=0, tiled=True),
-    )
+    send = jnp.concatenate([send_latent, send_back], axis=1)
+    send = send.reshape(group_count, local_count, capacity, 2 * width)
+    rows = lax.all_to_all(send, "expert", split_axis=0, concat_axis=0, tiled=True)
+    rows_latent = rows[..., :width]
+    rows_back = rows[..., width:]
     pre_gate = jnp.einsum(
         "neci,eih->nech", rows_latent, gate_full, preferred_element_type=jnp.float32
     )
@@ -97,11 +136,13 @@
     row_part = row_part + jnp.einsum(
         "nech,eih->neci", linear_delta, linear_full, preferred_element_type=jnp.float32
     )
-    row_whole = lax.psum(row_part, "half").astype(jnp.bfloat16)
-    returned = lax.all_to_all(row_whole, "expert", split_axis=0, concat_axis=0, tiled=True)
+    returned = lax.all_to_all(
+        row_part.astype(jnp.bfloat16), "expert", split_axis=0, concat_axis=0, tiled=True
+    )
     position = expert_ids * capacity + slot_ids
     gathered = returned.reshape(expert_count * capacity, width)[position]
-    latent_grad = jnp.sum(gathered.astype(jnp.float32), axis=1)
+    latent_half = jnp.sum(gathered.astype(jnp.float32), axis=1)
+    latent_grad = pair_sum(latent_half, 2)
     token_grad = lax.dot_general(
         latent_grad.astype(jnp.bfloat16),
         down_full,

time: 505 us -> 446 us (0.88)
  blocking collectives: 128 us -> 0 us
  waiting for transfers between devices: 195 us -> 243 us
  Pallas kernels: 0 us -> 42.2 us
  starting transfers between devices: 35.6 us -> 23.2 us
  matrix products: 65.5 us -> 56.6 us
    psum x2 -> x0, blocking collectives: 128 us -> none  [the longest x1 110 us: on_device(): row_whole = lax.psum(row_part, 'half').astype(jnp.bfloat16)]
    all_to_all x3 -> x2, waiting for transfers between devices: 95 us -> 205 us  [the longest x1 137 us: on_device(): lax.all_to_all(send, 'expert', split_axis=0, concat_axis=0, tiled=True)]
    psum x1 -> x0, waiting for transfers between devices: 49.1 us -> none  [on_device(): latent_sum, back_latent = lax.psum((latent_part, back_part), 'half')]
    pallas_call x0 -> x2, Pallas kernels: none -> 42.2 us  [pair_sum(): pl.pallas_call(_pair_sum_kernel, out_shape=jax.ShapeDtypeStruct(x.shape,...]
    all_gather x1, waiting for transfers between devices: 0.02 us -> 19.2 us  [on_device(): lax.all_gather(latent_up, 'dp', axis=0, tiled=True)]
    all_gather x1, waiting for transfers between devices: 16.9 us -> 0.01 us  [on_device(): lax.all_gather(expert_gate, 'dp', axis=1, tiled=True)]
    all_to_all x3 -> x2, starting transfers between devices: 34.5 us -> 22.5 us  [the longest x1 13 us: on_device(): lax.all_to_all(send, 'expert', split_axis=0, concat_axis=0, tiled=True)]
    all_gather x1, waiting for transfers between devices: 10.1 us -> 0.01 us  [on_device(): lax.all_gather(expert_linear, 'dp', axis=1, tiled=True)]
  transfers between devices with their start and end apart: 12 -> 10, of which waited for: 6 -> 4; matrix products, arithmetic and copies ran while one was open for 25% -> 18% of each run, Pallas kernels for 0% -> 3%
where the time goes in v1:
time: 446 us; the launch traced here: 438 us
  waiting for transfers between devices  243 us (54%)
  matrix products  56.6 us (13%)
  local copies, waits for them, and re-layouts  47.2 us (11%)
  Pallas kernels  42.2 us (9%)
  starting transfers between devices  23.2 us (5%)
  between operations  14.7 us (3%)
  other arithmetic  11.1 us (2%)
    all_to_all x1, waiting for transfers between devices, on_device(): lax.all_to_all(send, 'expert', split_axis=0, concat_axis=0, tiled=True)  137 us
    all_to_all x1, waiting for transfers between devices, on_device(): lax.all_to_all(row_part.astype(jnp.bfloat16), 'expert', split_axis=0, con...  67.9 us
    pallas_call x2, Pallas kernels, pair_sum(): pl.pallas_call(_pair_sum_kernel, out_shape=jax.ShapeDtypeStruct(x.shape,...  42.2 us
    all_gather x1, waiting for transfers between devices, on_device(): lax.all_gather(latent_up, 'dp', axis=0, tiled=True)  19.2 us
    all_gather x1, waiting for transfers between devices, on_device(): lax.all_gather(latent_down, 'dp', axis=1, tiled=True)  15.9 us
    all_to_all x1, starting transfers between devices, on_device(): lax.all_to_all(send, 'expert', split_axis=0, concat_axis=0, tiled=True)  13 us
    gather x2, local copies, waits for them, and re-layouts, on_device(): back_latent[token_of]  10.6 us
    dot_general x1, matrix products, on_device(): jnp.einsum('necj,ehj->nech', rows_back, output_full, preferred_element_ty...  10.5 us
  transfers between devices with their start and end apart: 10, of which 4 were waited for; matrix products, arithmetic and copies ran while one was open for 18% of the time, Pallas kernels for 3%

profile of v1, /device:TPU:64, one launch (start us, length us, event | category | flops | bytes accessed | tf_op | source)
XLA Modules:
  0.0 437.9 jit_solution(4067732763410916961)
XLA Ops:
  7.3 0.7 all-gather.6.cloned.1.call-update
  8.0 0.7 all-gather.8.cloned.1.call-update
  8.7 0.1 copy.29
  9.1 0.6 select_reduce_fusion
  9.8 4.6 %gather_fusion.1 = f32[1152]{0:T(1024)S(1)} fusion(f32[1024]{0:T(1024)S(1)} %reshape.179, s32[2048]{0:T(1024)S(1)} %get-tuple-element.12), kind=kCustom, calls=%fused_computation.1 | custom fusion | bytes 13824 | tf_op jit(solution)/shard_map/gather | solution.py:90
  14.3 0.1 mul.46
  14.5 0.6 fusion
  15.1 0.2 broadcast_in_dim.37
  15.2 15.9 %all-gather.6.cloned.1.call-done = bf16[2048,1024]{1,0:T(8,128)(2,1)} async-done(((bf16[2048,512]{1,0:T(8,128)(2,1)}), bf16[2048,1024]{1,0:T(8,128)(2,1)}) %all-gather.6.cloned.1.call-update) | async-done | bytes 4194320 | tf_op jit(solution)/shard_map/all_gather | solution.py:67
  31.1 2.9 fusion.41
  34.0 19.2 %all-gather.8.cloned.1.call-done = bf16[1024,2048]{1,0:T(8,128)(2,1)} async-done(((bf16[512,2048]{1,0:T(8,128)(2,1)}), bf16[1024,2048]{1,0:T(8,128)(2,1)}) %all-gather.8.cloned.1.call-update) | async-done | bytes 4194320 | tf_op jit(solution)/shard_map/all_gather | solution.py:68
  53.3 3.7 fusion.42
  57.0 1.1 pad_maximum_fusion.x_ref
  58.0 27.7 %shard_map.129 = f32[128,2048]{1,0:T(8,128)} custom-call(f32[128,2048]{1,0:T(8,128)} %pad_maximum_fusion.x_ref), custom_call_target="tpu_custom_call" | custom-call | tf_op jit(solution)/shard_map/pallas_call | solution.py:32
  85.7 1.1 slice.29
  86.9 5.0 %gather_fusion.2 = f32[1152,1024]{1,0:T(8,128)} fusion(f32[128,1024]{1,0:T(8,128)S(1)} %slice-done, s32[2048]{0:T(1024)S(1)} %get-tuple-element.13), kind=kCustom, calls=%fused_computation.2 | custom fusion | bytes 9441792 | tf_op jit(solution)/shard_map/gather | solution.py:92
  92.0 5.6 %gather.20 = f32[64,1,18,1024]{3,2,0,1:T(8,128)} reshape(f32[1152,1024]{1,0:T(8,128)} %gather_fusion.2) | data formatting | bytes 9437184 | tf_op jit(solution)/shard_map/gather | solution.py:92
  97.5 5.0 %gather_fusion = bf16[1152,1024]{1,0:T(8,128)(2,1)} fusion(bf16[128,1024]{1,0:T(8,128)(2,1)S(1)} %slice.29, s32[2048]{0:T(1024)S(1)} %get-tuple-element.13), kind=kCustom, calls=%fused_computation | custom fusion | bytes 4723200 | tf_op jit(solution)/shard_map/gather | solution.py:91
  102.5 2.7 gather.17
  105.3 0.4 broadcast_select_fusion
  105.7 2.4 copy-done.2
  108.0 0.7 select_convert_fusion
  108.8 3.8 maximum_bitcast_fusion
  112.5 13.0 %all-to-all-start = ((bf16[64,1,18,2048]{3,2,1,0:T(8,128)(2,1)}), bf16[64,1,18,2048]{3,2,1,0:T(8,128)(2,1)}, u32[]{:S(2)}, u32[]{:S(2)}) async-start(bf16[64,1,18,2048]{3,2,1,0:T(8,128)(2,1)} %maximum_bitcast_fusion), calls=%async_computation | async-start | bytes 12582912 | tf_op jit(solution)/shard_map/all_to_all | solution.py:97
  125.6 0.7 all-gather.12.cloned.1.call-update
  126.3 0.5 all-gather.14.cloned.1.call-update
  126.9 0.5 all-gather.10.cloned.1.call-update
  127.4 0.5 reduce-scatter.8.cloned.1.call-start
  127.9 136.7 %all-to-all-done = bf16[64,1,18,2048]{3,2,1,0:T(8,128)(2,1)} async-done(((bf16[64,1,18,2048]{3,2,1,0:T(8,128)(2,1)}), bf16[64,1,18,2048]{3,2,1,0:T(8,128)(2,1)}, u32[]{:S(2)}, u32[]{:S(2)}) %all-to-all-start) | async-done | bytes 4718624 | tf_op jit(solution)/shard_map/all_to_all | solution.py:97
  264.6 5.3 %fusion.40 = (bf16[64,1,18,1024]{3,2,1,0:T(8,128)(2,1)}, bf16[64,1,18,1024]{3,2,1,0:T(8,128)(2,1)S(1)}) fusion(bf16[64,1,18,2048]{3,2,1,0:T(8,128)(2,1)} %all-to-all-done), kind=kLoop, calls=%fused_computation.69 | loop fusion | bytes 9437184 | tf_op jit(solution)/shard_map/slice | solution.py:99
  269.9 7.2 %fusion.24 = f32[64,18,768]{2,0,1:T(8,128)} fusion(bf16[1,1024,768]{2,1,0:T(8,128)(2,1)} %all-gather.12.cloned.1.call-done, bf16[64,1,18,1024]{3,2,1,0:T(8,128)(2,1)S(1)} %get-tuple-element.11), kind=kOutput, calls=%fused_computation.46 | convolution fusion | flops 1811939328 | bytes 7471104 | tf_op jit(solution)/shard_map/neci,eih->nech/dot_general | solution.py:103
  277.2 5.6 %fusion.21 = f32[64,18,768]{2,0,1:T(8,128)S(1)} fusion(bf16[1,1024,768]{2,1,0:T(8,128)(2,1)} %all-gather.14.cloned.1.call-done, bf16[64,1,18,1024]{3,2,1,0:T(8,128)(2,1)S(1)} %get-tuple-element.11), kind=kOutput, calls=%fused_computation.43 | convolution fusion | flops 1811939328 | bytes 7471104 | tf_op jit(solution)/shard_map/neci,eih->nech/dot_general | solution.py:100
  282.8 1.7 copy-done.12
  284.5 5.9 %fusion.33 = bf16[1,768,1024]{2,1,0:T(8,128)(2,1)} fusion(bf16[64,1,18,1024]{3,2,1,0:T(8,128)(2,1)S(1)} %copy-done.3, f32[64,18,768]{2,0,1:T(8,128)S(1)} %copy-done.11, f32[64,18,768]{2,0,1:T(8,128)S(1)} %fusion.21), kind=kOutput, calls=%fused_computation.51 | convolution fusion | flops 1818034176 | bytes 11010048 | tf_op jit(solution)/shard_map/nech,necj->ehj/dot_general | solution.py:121
  290.5 10.5 %fusion.6 = (bf16[64,1,18,768]{3,0,2,1:T(8,128)(2,1)S(1)}, bf16[64,1,18,768]{3,0,2,1:T(8,128)(2,1)}) fusion(f32[64,18,768]{2,0,1:T(8,128)} %copy-done.12, f32[64,18,768]{2,0,1:T(8,128)} %fusion.24, bf16[1,768,1024]{2,1,0:T(8,128)(2,1)} %all-gather.10.cloned.1.call-done, bf16[64,1,18,1024]{3,2,1,0:T(8,128)(2,1)} %get-tuple-element.10), kind=kOutput, calls=%fused_computation.19 | convolution fusion | flops 1823440896 | bytes 14548992 | tf_op jit(solution)/shard_map/necj,ehj->nech/dot_general | solution.py:106
  301.0 1.2 copy-done.9
  302.3 4.2 fusion.30
  306.5 4.1 fusion.16
  310.7 2.0 fusion.11
  312.7 3.3 copy.34
  316.0 9.5 %all-to-all-start.1 = ((bf16[64,1,18,1024]{3,2,1,0:T(8,128)(2,1)}), bf16[64,1,18,1024]{3,2,1,0:T(8,128)(2,1)}, u32[]{:S(2)}, u32[]{:S(2)}) async-start(bf16[64,1,18,1024]{3,2,1,0:T(8,128)(2,1)} %copy.34), calls=%async_computation.1 | async-start | bytes 6291456 | tf_op jit(solution)/shard_map/all_to_all | solution.py:139
  325.6 5.7 %fusion.27 = bf16[1,1024,768]{2,1,0:T(8,128)(2,1)} fusion(bf16[64,1,18,768]{3,0,2,1:T(8,128)(2,1)} %get-tuple-element.9, bf16[64,1,18,1024]{3,2,1,0:T(8,128)(2,1)S(1)} %get-tuple-element.11), kind=kOutput, calls=%fused_computation.49 | convolution fusion | flops 1812725760 | bytes 5701632 | tf_op jit(solution)/shard_map/neci,nech->eih/dot_general | solution.py:115
  331.5 67.9 %all-to-all-done.1 = bf16[64,1,18,1024]{3,2,1,0:T(8,128)(2,1)} async-done(((bf16[64,1,18,1024]{3,2,1,0:T(8,128)(2,1)}), bf16[64,1,18,1024]{3,2,1,0:T(8,128)(2,1)}, u32[]{:S(2)}, u32[]{:S(2)}) %all-to-all-start.1) | async-done | bytes 2359328 | tf_op jit(solution)/shard_map/all_to_all | solution.py:139
  399.5 2.9 reshape.187
  402.4 5.4 %gather_fusion.3 = bf16[1024,1024]{1,0:T(8,128)(2,1)} fusion(bf16[1152,1024]{1,0:T(8,128)(2,1)S(1)} %reshape.187, s32[1024]{0:T(1024)S(1)} %broadcast_clamp_fusion), kind=kCustom, calls=%fused_computation.3 | custom fusion | bytes 4198400 | tf_op jit(solution)/shard_map/gather | solution.py:143
  407.8 3.8 convert_reduce_fusion.x_ref
  411.6 14.5 %shard_map.130 = f32[128,1024]{1,0:T(8,128)} custom-call(f32[128,1024]{1,0:T(8,128)} %convert_reduce_fusion.x_ref), custom_call_target="tpu_custom_call" | custom-call | tf_op jit(solution)/shard_map/pallas_call | solution.py:32
  426.1 4.7 %convolution_convert_fusion = bf16[128,2048]{1,0:T(8,128)(2,1)} fusion(bf16[2048,1024]{1,0:T(8,128)(2,1)} %all-gather.6.cloned.1.call-done, f32[128,1024]{1,0:T(8,128)} %shard_map.130), kind=kOutput, calls=%fused_computation.31 | convolution fusion | flops 537264128 | bytes 5242880 | tf_op jit(solution)/shard_map/dot_general | solution.py:146
  (50 shorter events, 1.0 us)
Async XLA Ops:
  7.2 24.0 %copy-start = (bf16[128,2048]{1,0:T(8,128)(2,1)S(1)}, bf16[128,2048]{1,0:T(8,128)(2,1)}, u32[]{:S(2)}) copy-start(bf16[128,2048]{1,0:T(8,128)(2,1)} %param.10) | copy-start | bytes 1572868
  7.2 1.5 copy-start.7
  7.2 1.5 copy-start.6
  7.2 1.7 copy-start.5
  7.2 23.9 %all-gather.6.cloned.1.call-start = ((), (), s32[]{:S(2)}) async-start(), calls=%async_computation.5 | async-start | bytes 6291456 | tf_op jit(solution)/shard_map/all_gather | solution.py:67
  7.9 45.3 %all-gather.8.cloned.1.call-start = ((), (), s32[]{:S(2)}) async-start(), calls=%async_computation.6 | async-start | bytes 6291456 | tf_op jit(solution)/shard_map/all_gather | solution.py:68
  14.3 38.9 %copy-start.4 = (bf16[128,2048]{1,0:T(8,128)(2,1)S(1)}, bf16[128,2048]{1,0:T(8,128)(2,1)}, u32[]{:S(2)}) copy-start(bf16[128,2048]{1,0:T(8,128)(2,1)} %param.11) | copy-start | bytes 1572868
  85.7 1.2 slice-start
  105.2 2.8 copy-start.2
  112.5 152.1 %all-to-all-start = ((bf16[64,1,18,2048]{3,2,1,0:T(8,128)(2,1)}), bf16[64,1,18,2048]{3,2,1,0:T(8,128)(2,1)}, u32[]{:S(2)}, u32[]{:S(2)}) async-start(bf16[64,1,18,2048]{3,2,1,0:T(8,128)(2,1)} %maximum_bitcast_fusion), calls=%async_computation | async-start | bytes 12582912 | tf_op jit(solution)/shard_map/all_to_all | solution.py:97
  125.5 144.4 %all-gather.12.cloned.1.call-start = ((), (), s32[]{:S(2)}) async-start(), calls=%async_computation.8 | async-start | bytes 2359296 | tf_op jit(solution)/shard_map/all_gather | solution.py:70
  126.3 150.9 %all-gather.14.cloned.1.call-start = ((), (), s32[]{:S(2)}) async-start(), calls=%async_computation.9 | async-start | bytes 2359296 | tf_op jit(solution)/shard_map/all_gather | solution.py:69
  126.8 163.6 %all-gather.10.cloned.1.call-start = ((), (), s32[]{:S(2)}) async-start(), calls=%async_computation.7 | async-start | bytes 2359296 | tf_op jit(solution)/shard_map/all_gather | solution.py:71
  127.4 303.4 %reduce-scatter.8.cloned.1.call-start = ((), (), s32[]{:S(2)}) async-start(), calls=%async_computation.12 | async-start | bytes 2359296 | tf_op jit(solution)/shard_map/reduce_scatter | solution.py:129
  277.2 7.4 %copy-start.3 = (bf16[64,1,18,1024]{3,2,1,0:T(8,128)(2,1)S(1)}, bf16[64,1,18,1024]{3,2,1,0:T(8,128)(2,1)}, u32[]{:S(2)}) copy-start(bf16[64,1,18,1024]{3,2,1,0:T(8,128)(2,1)} %get-tuple-element.10) | copy-start | bytes 7077892
  277.2 7.4 %copy-start.11 = (f32[64,18,768]{2,0,1:T(8,128)S(1)}, f32[64,18,768]{2,0,1:T(8,128)}, u32[]{:S(2)}) copy-start(f32[64,18,768]{2,0,1:T(8,128)} %fusion.24) | copy-start | bytes 10616836
  282.8 1.8 copy-start.12
  290.4 140.4 %reduce-scatter.6.cloned.1.call-start = ((), (), s32[]{:S(2)}) async-start(), calls=%async_computation.11 | async-start | bytes 2359296 | tf_op jit(solution)/shard_map/reduce_scatter | solution.py:126
  301.0 1.2 copy-start.9
  306.5 4.2 copy-start.8
  306.5 4.2 copy-start.10
  316.0 83.5 %all-to-all-start.1 = ((bf16[64,1,18,1024]{3,2,1,0:T(8,128)(2,1)}), bf16[64,1,18,1024]{3,2,1,0:T(8,128)(2,1)}, u32[]{:S(2)}, u32[]{:S(2)}) async-start(bf16[64,1,18,1024]{3,2,1,0:T(8,128)(2,1)} %copy.34), calls=%async_computation.1 | async-start | bytes 6291456 | tf_op jit(solution)/shard_map/all_to_all | solution.py:139
  325.5 105.3 %reduce-scatter.4.cloned.1.call-start = ((), (), s32[]{:S(2)}) async-start(), calls=%async_computation.10 | async-start | bytes 2359296 | tf_op jit(solution)/shard_map/reduce_scatter | solution.py:123
  407.8 23.0 %copy-start.1 = (bf16[128,2048]{1,0:T(8,128)(2,1)S(1)}, bf16[128,2048]{1,0:T(8,128)(2,1)}, u32[]{:S(2)}) copy-start(bf16[128,2048]{1,0:T(8,128)(2,1)} %param.10) | copy-start | bytes 1572868
Sparse Core Ops, SparseCore 0:
  9.8 21.2 all-gather.5
  32.9 20.2 all-gather.7
  128.2 16.4 all-gather.11
  146.3 16.4 all-gather.13
  164.4 16.4 all-gather.9
  290.5 12.2 reduce-scatter.7
  306.6 15.0 reduce-scatter.5
  331.4 15.6 reduce-scatter.3

commit v2 on v1

--- a/solution.py
+++ b/solution.py
@@ -41,6 +41,73 @@
         ],
         compiler_params=pltpu.CompilerParams(collective_id=collective_id, has_side_effects=True),
     )(x)
+
+
+def _all_to_all_kernel(x_ref, o_ref, send_sem, recv_sem, local_sem):
+    count = x_ref.shape[0]
+    me = lax.axis_index("expert")
+    barrier = pltpu.get_barrier_semaphore()
+
+    def greet(step, carry):
+        peer = lax.rem(me + step, count)
+        pl.semaphore_signal(barrier, inc=1, device_id={"expert": peer}, device_id_type=MESH)
+        return carry
+
+    lax.fori_loop(1, count, greet, 0)
+    pl.semaphore_wait(barrier, count - 1)
+    local = pltpu.make_async_copy(x_ref.at[me], o_ref.at[me], local_sem)
+    local.start()
+
+    def remote(peer):
+        return pltpu.make_async_remote_copy(
+            src_ref=x_ref.at[peer],
+            dst_ref=o_ref.at[me],
+            send_sem=send_sem.at[peer],
+            recv_sem=recv_sem.at[me],
+            device_id={"expert": peer},
+            device_id_type=MESH,
+        )
+
+    def send(step, carry):
+        remote(lax.rem(me + step, count)).start()
+        return carry
+
+    lax.fori_loop(1, count, send, 0)
+
+    def drain(step, carry):
+        peer = lax.rem(me + step, count)
+        remote(peer).wait_send()
+        pltpu.make_async_remote_copy(
+            src_ref=x_ref.at[peer],
+            dst_ref=o_ref.at[peer],
+            send_sem=send_sem.at[peer],
+            recv_sem=recv_sem.at[peer],
+            device_id={"expert": peer},
+            device_id_type=MESH,
+        ).wait_recv()
+        return carry
+
+    lax.fori_loop(1, count, drain, 0)
+    local.wait()
+
+
+def all_to_all_kernel(x, collective_id):
+    count = lax.axis_size("expert")
+    shape = x.shape
+    blocks = x.reshape(count, -1, shape[-1])
+    out = pl.pallas_call(
+        _all_to_all_kernel,
+        out_shape=jax.ShapeDtypeStruct(blocks.shape, blocks.dtype),
+        in_specs=[pl.BlockSpec(memory_space=pl.ANY)],
+        out_specs=pl.BlockSpec(memory_space=pl.ANY),
+        scratch_shapes=[
+            pltpu.SemaphoreType.DMA((count,)),
+            pltpu.SemaphoreType.DMA((count,)),
+            pltpu.SemaphoreType.DMA(()),
+        ],
+        compiler_params=pltpu.CompilerParams(collective_id=collective_id, has_side_effects=True),
+    )(blocks)
+    return out.reshape(shape)
 
 
 def on_device(
@@ -94,7 +161,7 @@
     )
     send = jnp.concatenate([send_latent, send_back], axis=1)
     send = send.reshape(group_count, local_count, capacity, 2 * width)
-    rows = lax.all_to_all(send, "expert", split_axis=0, concat_axis=0, tiled=True)
+    rows = all_to_all_kernel(send, 3)
     rows_latent = rows[..., :width]
     rows_back = rows[..., width:]
     pre_gate = jnp.einsum(
@@ -136,9 +203,7 @@
     row_part = row_part + jnp.einsum(
         "nech,eih->neci", linear_delta, linear_full, preferred_element_type=jnp.float32
     )
-    returned = lax.all_to_all(
-        row_part.astype(jnp.bfloat16), "expert", split_axis=0, concat_axis=0, tiled=True
-    )
+    returned = all_to_all_kernel(row_part.astype(jnp.bfloat16), 4)
     position = expert_ids * capacity + slot_ids
     gathered = returned.reshape(expert_count * capacity, width)[position]
     latent_half = jnp.sum(gathered.astype(jnp.float32), axis=1)

time: 446 us -> 444 us (level)
  Pallas kernels: 42.2 us -> 271 us
  waiting for transfers between devices: 243 us -> 36.4 us
  starting transfers between devices: 23.2 us -> 0.52 us
    pallas_call x0 -> x2, Pallas kernels: none -> 229 us  [all_to_all_kernel(): pl.pallas_call(_all_to_all_kernel, out_shape=jax.ShapeDtypeStruct(blocks....]
    all_to_all x2 -> x0, waiting for transfers between devices: 205 us -> none  [the longest x1 137 us: on_device(): lax.all_to_all(send, 'expert', split_axis=0, concat_axis=0, tiled=True)]
    all_to_all x2 -> x0, starting transfers between devices: 22.5 us -> none  [the longest x1 13 us: on_device(): lax.all_to_all(send, 'expert', split_axis=0, concat_axis=0, tiled=True)]
    another operation x0 -> x2, local copies, waits for them, and re-layouts: none -> 8.23 us
    slice x1 -> x0, local copies, waits for them, and re-layouts: 5.3 us -> none  [on_device(): rows_back = rows[..., width:]]
  transfers between devices with their start and end apart: 10 -> 8, of which waited for: 4 -> 2; matrix products, arithmetic and copies ran while one was open for 18% -> 25% of each run, Pallas kernels for 3% -> 62%
where the time goes in v2:
time: 444 us; the launch traced here: 438 us
  Pallas kernels  271 us (61%)
  matrix products  56.6 us (13%)
  local copies, waits for them, and re-layouts  47.5 us (11%)
  waiting for transfers between devices  36.4 us (8%)
  between operations  14.7 us (3%)
  other arithmetic  11.1 us (2%)
    pallas_call x2, Pallas kernels, all_to_all_kernel(): pl.pallas_call(_all_to_all_kernel, out_shape=jax.ShapeDtypeStruct(blocks....  229 us
    pallas_call x2, Pallas kernels, pair_sum(): pl.pallas_call(_pair_sum_kernel, out_shape=jax.ShapeDtypeStruct(x.shape,...  41.9 us
    all_gather x1, waiting for transfers between devices, on_device(): lax.all_gather(latent_up, 'dp', axis=0, tiled=True)  19.2 us
    all_gather x1, waiting for transfers between devices, on_device(): lax.all_gather(latent_down, 'dp', axis=1, tiled=True)  13.9 us
    gather x2, local copies, waits for them, and re-layouts, on_device(): back_latent[token_of]  10.7 us
    dot_general x1, matrix products, on_device(): jnp.einsum('necj,ehj->nech', rows_back, output_full, preferred_element_ty...  10.5 us
  transfers between devices with their start and end apart: 8, of which 2 were waited for; matrix products, arithmetic and copies ran while one was open for 25% of the time, Pallas kernels for 62%

profile of v2, /device:TPU:64, one launch (start us, length us, event | category | flops | bytes accessed | tf_op | source)
XLA Modules:
  0.0 437.8 jit_solution(17837050624680734803)
XLA Ops:
  7.3 0.7 all-gather.6.cloned.1.call-update
  8.0 0.7 all-gather.8.cloned.1.call-update
  8.7 0.7 all-gather.12.cloned.1.call-update
  9.5 0.5 all-gather.14.cloned.1.call-update
  10.1 0.5 all-gather.10.cloned.1.call-update
  10.7 0.1 copy.44
  10.9 0.6 select_reduce_fusion
  11.4 0.6 fusion
  12.1 0.1 copy.45
  12.3 4.6 %gather_fusion.1 = f32[1152]{0:T(1024)S(1)} fusion(f32[1024]{0:T(1024)S(1)} %reshape.149, s32[2048]{0:T(1024)S(1)} %get-tuple-element.12), kind=kCustom, calls=%fused_computation.1 | custom fusion | bytes 13824 | tf_op jit(solution)/shard_map/gather | solution.py:157
  16.9 0.1 mul.40
  17.0 0.2 broadcast_in_dim.37
  17.2 13.9 %all-gather.6.cloned.1.call-done = bf16[2048,1024]{1,0:T(8,128)(2,1)} async-done(((bf16[2048,512]{1,0:T(8,128)(2,1)}), bf16[2048,1024]{1,0:T(8,128)(2,1)}) %all-gather.6.cloned.1.call-update) | async-done | bytes 4194320 | tf_op jit(solution)/shard_map/all_gather | solution.py:134
  31.1 2.9 fusion.47
  34.0 19.2 %all-gather.8.cloned.1.call-done = bf16[1024,2048]{1,0:T(8,128)(2,1)} async-done(((bf16[512,2048]{1,0:T(8,128)(2,1)}), bf16[1024,2048]{1,0:T(8,128)(2,1)}) %all-gather.8.cloned.1.call-update) | async-done | bytes 4194320 | tf_op jit(solution)/shard_map/all_gather | solution.py:135
  53.3 3.7 fusion.48
  57.0 1.1 pad_maximum_fusion.1.x_ref
  58.0 27.7 %shard_map.129 = f32[128,2048]{1,0:T(8,128)} custom-call(f32[128,2048]{1,0:T(8,128)} %pad_maximum_fusion.1.x_ref), custom_call_target="tpu_custom_call" | custom-call | tf_op jit(solution)/shard_map/pallas_call | solution.py:32
  85.8 1.2 slice.31
  87.0 5.1 %gather_fusion.2 = f32[1152,1024]{1,0:T(8,128)} fusion(f32[128,1024]{1,0:T(8,128)S(1)} %slice-done, s32[2048]{0:T(1024)S(1)} %get-tuple-element.13), kind=kCustom, calls=%fused_computation.2 | custom fusion | bytes 9441792 | tf_op jit(solution)/shard_map/gather | solution.py:159
  92.1 5.6 %gather.20 = f32[64,18,1024]{2,1,0:T(8,128)} reshape(f32[1152,1024]{1,0:T(8,128)} %gather_fusion.2) | data formatting | bytes 9437184 | tf_op jit(solution)/shard_map/gather | solution.py:159
  97.7 5.0 %gather_fusion = bf16[1152,1024]{1,0:T(8,128)(2,1)} fusion(bf16[128,1024]{1,0:T(8,128)(2,1)S(1)} %slice.31, s32[2048]{0:T(1024)S(1)} %get-tuple-element.13), kind=kCustom, calls=%fused_computation | custom fusion | bytes 4723200 | tf_op jit(solution)/shard_map/gather | solution.py:158
  102.7 2.8 gather.17
  105.5 0.4 broadcast_select_fusion
  105.9 2.6 copy-done.2
  108.5 0.7 select_convert_fusion
  109.3 3.8 pad_maximum_fusion.x_ref
  113.1 150.9 %shard_map.130 = bf16[64,18,2048]{2,1,0:T(8,128)(2,1)} custom-call(bf16[64,18,2048]{2,1,0:T(8,128)(2,1)} %pad_maximum_fusion.x_ref), custom_call_target="tpu_custom_call" | custom-call | tf_op jit(solution)/shard_map/pallas_call | solution.py:98
  264.0 5.3 %slice_bitcast_fusion.1 = (bf16[64,18,1024]{2,1,0:T(8,128)(2,1)}, bf16[64,18,1024]{2,1,0:T(8,128)(2,1)S(1)}) fusion(bf16[64,1,18,2048]{3,2,0,1:T(8,128)(2,1)} %bitcast.131), kind=kLoop, calls=%fused_computation.28 | loop fusion | bytes 9437184 | tf_op jit(solution)/shard_map/reshape.1
  269.3 7.2 %fusion.25 = f32[64,18,768]{2,0,1:T(8,128)} fusion(bf16[1,1024,768]{2,1,0:T(8,128)(2,1)} %all-gather.12.cloned.1.call-done, bf16[64,18,1024]{2,1,0:T(8,128)(2,1)S(1)} %get-tuple-element.11), kind=kOutput, calls=%fused_computation.48 | convolution fusion | flops 1811939328 | bytes 7471104 | tf_op jit(solution)/shard_map/neci,eih->nech/dot_general | solution.py:170
  276.5 5.6 %fusion.22 = f32[64,18,768]{2,0,1:T(8,128)S(1)} fusion(bf16[1,1024,768]{2,1,0:T(8,128)(2,1)} %all-gather.14.cloned.1.call-done, bf16[64,18,1024]{2,1,0:T(8,128)(2,1)S(1)} %get-tuple-element.11), kind=kOutput, calls=%fused_computation.45 | convolution fusion | flops 1811939328 | bytes 7471104 | tf_op jit(solution)/shard_map/neci,eih->nech/dot_general | solution.py:167
  282.1 1.7 copy-done.12
  283.9 5.9 %fusion.34 = bf16[1,768,1024]{2,1,0:T(8,128)(2,1)} fusion(bf16[64,18,1024]{2,1,0:T(8,128)(2,1)S(1)} %copy-done.3, f32[64,18,768]{2,0,1:T(8,128)S(1)} %copy-done.11, f32[64,18,768]{2,0,1:T(8,128)S(1)} %fusion.22), kind=kOutput, calls=%fused_computation.53 | convolution fusion | flops 1818034176 | bytes 11010048 | tf_op jit(solution)/shard_map/nech,necj->ehj/dot_general | solution.py:188
  289.8 10.5 %fusion.6 = (bf16[64,1,18,768]{3,0,2,1:T(8,128)(2,1)S(1)}, bf16[64,1,18,768]{3,0,2,1:T(8,128)(2,1)}) fusion(f32[64,18,768]{2,0,1:T(8,128)} %copy-done.12, f32[64,18,768]{2,0,1:T(8,128)} %fusion.25, bf16[1,768,1024]{2,1,0:T(8,128)(2,1)} %all-gather.10.cloned.1.call-done, bf16[64,18,1024]{2,1,0:T(8,128)(2,1)} %get-tuple-element.10), kind=kOutput, calls=%fused_computation.19 | convolution fusion | flops 1823440896 | bytes 14548992 | tf_op jit(solution)/shard_map/necj,ehj->nech/dot_general | solution.py:173
  300.4 1.2 copy-done.9
  301.6 4.3 fusion.31
  306.0 0.3 reduce-scatter.4.cloned.1.call-start
  306.2 5.7 %fusion.28 = bf16[1,1024,768]{2,1,0:T(8,128)(2,1)} fusion(bf16[64,1,18,768]{3,0,2,1:T(8,128)(2,1)} %get-tuple-element.9, bf16[64,18,1024]{2,1,0:T(8,128)(2,1)S(1)} %get-tuple-element.11), kind=kOutput, calls=%fused_computation.51 | convolution fusion | flops 1812725760 | bytes 5701632 | tf_op jit(solution)/shard_map/neci,nech->eih/dot_general | solution.py:182
  311.9 0.1 copy.50
  312.1 4.1 fusion.15
  316.3 2.0 convolution_add_fusion
  318.3 3.0 copy.69.x_ref
  321.4 78.4 %shard_map.131 = bf16[64,18,1024]{2,1,0:T(8,128)(2,1)} custom-call(bf16[64,18,1024]{2,1,0:T(8,128)(2,1)} %copy.69.x_ref), custom_call_target="tpu_custom_call" | custom-call | tf_op jit(solution)/shard_map/pallas_call | solution.py:98
  399.8 2.9 reshape_reshape.4
  402.7 5.4 %gather_fusion.3 = bf16[1024,1024]{1,0:T(8,128)(2,1)} fusion(bf16[1152,1024]{1,0:T(8,128)(2,1)S(1)} %reshape_reshape.4, s32[1024]{0:T(1024)S(1)} %broadcast_clamp_fusion), kind=kCustom, calls=%fused_computation.3 | custom fusion | bytes 4198400 | tf_op jit(solution)/shard_map/gather | solution.py:208
  408.1 3.8 convert_reduce_fusion.x_ref
  411.9 14.2 %shard_map.132 = f32[128,1024]{1,0:T(8,128)} custom-call(f32[128,1024]{1,0:T(8,128)} %convert_reduce_fusion.x_ref), custom_call_target="tpu_custom_call" | custom-call | tf_op jit(solution)/shard_map/pallas_call | solution.py:32
  426.1 4.7 %convolution_convert_fusion = bf16[128,2048]{1,0:T(8,128)(2,1)} fusion(bf16[2048,1024]{1,0:T(8,128)(2,1)} %all-gather.6.cloned.1.call-done, f32[128,1024]{1,0:T(8,128)} %shard_map.132), kind=kOutput, calls=%fused_computation.33 | convolution fusion | flops 537264128 | bytes 5242880 | tf_op jit(solution)/shard_map/dot_general | solution.py:211
  (48 shorter events, 0.8 us)
Async XLA Ops:
  7.2 24.0 %copy-start = (bf16[128,2048]{1,0:T(8,128)(2,1)S(1)}, bf16[128,2048]{1,0:T(8,128)(2,1)}, u32[]{:S(2)}) copy-start(bf16[128,2048]{1,0:T(8,128)(2,1)} %param.10) | copy-start | bytes 1572868
  7.2 3.5 copy-start.7
  7.2 3.5 copy-start.6
  7.2 4.9 %copy-start.5 = (f32[128,8]{0,1:T(8,128)S(1)}, f32[128,8]{0,1:T(8,128)}, u32[]{:S(2)}) copy-start(f32[128,8]{0,1:T(8,128)} %param.14) | copy-start | bytes 12292
  7.2 23.9 %all-gather.6.cloned.1.call-start = ((), (), s32[]{:S(2)}) async-start(), calls=%async_computation.3 | async-start | bytes 6291456 | tf_op jit(solution)/shard_map/all_gather | solution.py:134
  7.9 45.3 %all-gather.8.cloned.1.call-start = ((), (), s32[]{:S(2)}) async-start(), calls=%async_computation.4 | async-start | bytes 6291456 | tf_op jit(solution)/shard_map/all_gather | solution.py:135
  8.7 260.6 %all-gather.12.cloned.1.call-start = ((), (), s32[]{:S(2)}) async-start(), calls=%async_computation.6 | async-start | bytes 2359296 | tf_op jit(solution)/shard_map/all_gather | solution.py:137
  9.4 267.1 %all-gather.14.cloned.1.call-start = ((), (), s32[]{:S(2)}) async-start(), calls=%async_computation.7 | async-start | bytes 2359296 | tf_op jit(solution)/shard_map/all_gather | solution.py:136
  10.0 279.8 %all-gather.10.cloned.1.call-start = ((), (), s32[]{:S(2)}) async-start(), calls=%async_computation.5 | async-start | bytes 2359296 | tf_op jit(solution)/shard_map/all_gather | solution.py:138
  10.6 420.2 %reduce-scatter.8.cloned.1.call-start = ((), (), s32[]{:S(2)}) async-start(), calls=%async_computation.10 | async-start | bytes 2359296 | tf_op jit(solution)/shard_map/reduce_scatter | solution.py:196
  16.9 36.4 %copy-start.4 = (bf16[128,2048]{1,0:T(8,128)(2,1)S(1)}, bf16[128,2048]{1,0:T(8,128)(2,1)}, u32[]{:S(2)}) copy-start(bf16[128,2048]{1,0:T(8,128)(2,1)} %param.11) | copy-start | bytes 1572868
  85.7 1.3 slice-start
  105.5 3.0 copy-start.2
  276.5 7.4 %copy-start.3 = (bf16[64,18,1024]{2,1,0:T(8,128)(2,1)S(1)}, bf16[64,18,1024]{2,1,0:T(8,128)(2,1)}, u32[]{:S(2)}) copy-start(bf16[64,18,1024]{2,1,0:T(8,128)(2,1)} %get-tuple-element.10) | copy-start | bytes 7077892
  276.5 7.4 %copy-start.11 = (f32[64,18,768]{2,0,1:T(8,128)S(1)}, f32[64,18,768]{2,0,1:T(8,128)}, u32[]{:S(2)}) copy-start(f32[64,18,768]{2,0,1:T(8,128)} %fusion.25) | copy-start | bytes 10616836
  282.1 1.8 copy-start.12
  289.7 141.0 %reduce-scatter.6.cloned.1.call-start = ((), (), s32[]{:S(2)}) async-start(), calls=%async_computation.9 | async-start | bytes 2359296 | tf_op jit(solution)/shard_map/reduce_scatter | solution.py:193
  300.4 1.2 copy-start.9
  306.0 124.8 %reduce-scatter.4.cloned.1.call-start = ((), (), s32[]{:S(2)}) async-start(), calls=%async_computation.8 | async-start | bytes 2359296 | tf_op jit(solution)/shard_map/reduce_scatter | solution.py:190
  312.1 4.1 copy-start.8
  312.1 4.1 copy-start.10
  408.1 22.7 %copy-start.1 = (bf16[128,2048]{1,0:T(8,128)(2,1)S(1)}, bf16[128,2048]{1,0:T(8,128)(2,1)}, u32[]{:S(2)}) copy-start(bf16[128,2048]{1,0:T(8,128)(2,1)} %param.10) | copy-start | bytes 1572868
Sparse Core Ops, SparseCore 0:
  9.8 21.2 all-gather.5
  32.9 20.2 all-gather.7
  55.1 16.4 all-gather.11
  73.2 16.4 all-gather.13
  91.3 16.4 all-gather.9
  289.9 11.2 reduce-scatter.7
  306.1 14.0 reduce-scatter.5
  323.3 15.6 reduce-scatter.3

commit v3 on v2

--- a/solution.py
+++ b/solution.py
@@ -145,11 +145,17 @@
     both = pair_sum(jnp.concatenate([latent_part, back_part], axis=1), 1)
     latent = both[:, :width].astype(jnp.bfloat16)
     back_latent = both[:, width:]
+    half_cap = capacity // 2
+    side = lax.axis_index("half")
+    swap = [(0, 1), (1, 0)]
     flat_slot = (expert_ids * capacity + slot_ids).reshape(-1)
-    slot_table = lax.broadcasted_iota(
-        jnp.int32, (expert_count * capacity, row_count * pick_count), 0
-    )
-    matches = flat_slot[None, :] == slot_table
+    owned_shape = (expert_count, half_cap)
+    owned_slot = (
+        lax.broadcasted_iota(jnp.int32, owned_shape, 0) * capacity
+        + side * half_cap
+        + lax.broadcasted_iota(jnp.int32, owned_shape, 1)
+    ).reshape(-1)
+    matches = flat_slot[None, :] == owned_slot[:, None]
     choice_index = lax.broadcasted_iota(jnp.int32, matches.shape, 1)
     source = jnp.sum(jnp.where(matches, choice_index, 0), axis=1)
     filled = jnp.any(matches, axis=1)
@@ -160,32 +166,57 @@
         jnp.bfloat16
     )
     send = jnp.concatenate([send_latent, send_back], axis=1)
-    send = send.reshape(group_count, local_count, capacity, 2 * width)
-    rows = all_to_all_kernel(send, 3)
-    rows_latent = rows[..., :width]
-    rows_back = rows[..., width:]
-    pre_gate = jnp.einsum(
-        "neci,eih->nech", rows_latent, gate_full, preferred_element_type=jnp.float32
-    )
-    pre_linear = jnp.einsum(
-        "neci,eih->nech", rows_latent, linear_full, preferred_element_type=jnp.float32
-    )
-    grad_hidden = jnp.einsum(
-        "necj,ehj->nech", rows_back, output_full, preferred_element_type=jnp.float32
-    )
-    logistic = jax.nn.sigmoid(pre_gate)
-    hidden = (pre_gate * logistic * pre_linear).astype(jnp.bfloat16)
-    gate_delta = (grad_hidden * pre_linear * logistic * (1.0 + pre_gate * (1.0 - logistic))).astype(
-        jnp.bfloat16
-    )
-    linear_delta = (grad_hidden * pre_gate * logistic).astype(jnp.bfloat16)
-    gate_part = jnp.einsum(
-        "neci,nech->eih", rows_latent, gate_delta, preferred_element_type=jnp.float32
-    )
-    linear_part = jnp.einsum(
-        "neci,nech->eih", rows_latent, linear_delta, preferred_element_type=jnp.float32
-    )
-    out_part = jnp.einsum("nech,necj->ehj", hidden, rows_back, preferred_element_type=jnp.float32)
+    send = send.reshape(group_count, local_count, half_cap, 2 * width)
+    mine = all_to_all_kernel(send, 3)
+    theirs = lax.ppermute(mine, "half", swap)
+
+    def forward(rows):
+        rows_latent = rows[..., :width]
+        rows_back = rows[..., width:]
+        pre_gate = jnp.einsum(
+            "neci,eih->nech", rows_latent, gate_full, preferred_element_type=jnp.float32
+        )
+        pre_linear = jnp.einsum(
+            "neci,eih->nech", rows_latent, linear_full, preferred_element_type=jnp.float32
+        )
+        grad_hidden = jnp.einsum(
+            "necj,ehj->nech", rows_back, output_full, preferred_element_type=jnp.float32
+        )
+        logistic = jax.nn.sigmoid(pre_gate)
+        hidden = (pre_gate * logistic * pre_linear).astype(jnp.bfloat16)
+        gate_delta = (
+            grad_hidden * pre_linear * logistic * (1.0 + pre_gate * (1.0 - logistic))
+        ).astype(jnp.bfloat16)
+        linear_delta = (grad_hidden * pre_gate * logistic).astype(jnp.bfloat16)
+        return rows_latent, rows_back, hidden, gate_delta, linear_delta
+
+    def row_grad(gate_delta, linear_delta):
+        row_part = jnp.einsum(
+            "nech,eih->neci", gate_delta, gate_full, preferred_element_type=jnp.float32
+        )
+        return row_part + jnp.einsum(
+            "nech,eih->neci", linear_delta, linear_full, preferred_element_type=jnp.float32
+        )
+
+    def weight_grads(rows_latent, rows_back, hidden, gate_delta, linear_delta):
+        gate_part = jnp.einsum(
+            "neci,nech->eih", rows_latent, gate_delta, preferred_element_type=jnp.float32
+        )
+        linear_part = jnp.einsum(
+            "neci,nech->eih", rows_latent, linear_delta, preferred_element_type=jnp.float32
+        )
+        out_part = jnp.einsum(
+            "nech,necj->ehj", hidden, rows_back, preferred_element_type=jnp.float32
+        )
+        return gate_part, linear_part, out_part
+
+    own = forward(mine)
+    other = forward(theirs)
+    other_rows = lax.ppermute(row_grad(other[3], other[4]).astype(jnp.bfloat16), "half", swap)
+    own_rows = row_grad(own[3], own[4]) + other_rows.astype(jnp.float32)
+    own_parts = weight_grads(*own)
+    other_parts = weight_grads(*other)
+    gate_part, linear_part, out_part = (a + b for a, b in zip(own_parts, other_parts))
     gate_share, linear_share, out_share = (
         lax.psum_scatter(
             gate_part.astype(jnp.bfloat16), "dp", scatter_dimension=1, tiled=True
@@ -197,16 +228,12 @@
             out_part.astype(jnp.bfloat16), "dp", scatter_dimension=2, tiled=True
         ).astype(jnp.float32),
     )
-    row_part = jnp.einsum(
-        "nech,eih->neci", gate_delta, gate_full, preferred_element_type=jnp.float32
-    )
-    row_part = row_part + jnp.einsum(
-        "nech,eih->neci", linear_delta, linear_full, preferred_element_type=jnp.float32
-    )
-    returned = all_to_all_kernel(row_part.astype(jnp.bfloat16), 4)
-    position = expert_ids * capacity + slot_ids
-    gathered = returned.reshape(expert_count * capacity, width)[position]
-    latent_half = jnp.sum(gathered.astype(jnp.float32), axis=1)
+    returned = all_to_all_kernel(own_rows.astype(jnp.bfloat16), 4)
+    slot_rel = slot_ids - side * half_cap
+    owned = (slot_rel >= 0) & (slot_rel < half_cap)
+    position = expert_ids * half_cap + jnp.clip(slot_rel, 0, half_cap - 1)
+    gathered = returned.reshape(expert_count * half_cap, width)[position]
+    latent_half = jnp.sum(jnp.where(owned[..., None], gathered.astype(jnp.float32), 0.0), axis=1)
     latent_grad = pair_sum(latent_half, 2)
     token_grad = lax.dot_general(
         latent_grad.astype(jnp.bfloat16),

time: 444 us -> 426 us (0.959)
  Pallas kernels: 271 us -> 201 us
  waiting for transfers between devices: 36.4 us -> 95.9 us
  local copies, waits for them, and re-layouts: 47.5 us -> 33.6 us
    pallas_call x2, Pallas kernels: 229 us -> 160 us  [all_to_all_kernel(): pl.pallas_call(_all_to_all_kernel, out_shape=jax.ShapeDtypeStruct(blocks....]
    ppermute x0 -> x2, waiting for transfers between devices: none -> 57.4 us  [the longest x1 36.8 us: on_device(): theirs = lax.ppermute(mine, 'half', swap)]
    gather x2, local copies, waits for them, and re-layouts: 10.7 us -> 4.68 us  [on_device(): back_latent[token_of]]
    dot_general x8 -> x16, matrix products: 45.4 us -> 47.8 us  [the longest x2 8.82 us: forward(): jnp.einsum('necj,ehj->nech', rows_back, output_full, preferred_element_ty...]
  transfers between devices with their start and end apart: 8 -> 10, of which waited for: 2 -> 4; matrix products, arithmetic and copies ran while one was open for 25% -> 24% of each run, Pallas kernels for 62% -> 48%
where the time goes in v3:
time: 426 us; the launch traced here: 417 us
  Pallas kernels  201 us (47%)
  waiting for transfers between devices  95.9 us (23%)
  matrix products  59.1 us (14%)
  local copies, waits for them, and re-layouts  33.6 us (8%)
  between operations  14.9 us (3%)
  other arithmetic  11 us (3%)
    pallas_call x2, Pallas kernels, all_to_all_kernel(): pl.pallas_call(_all_to_all_kernel, out_shape=jax.ShapeDtypeStruct(blocks....  160 us
    pallas_call x2, Pallas kernels, pair_sum(): pl.pallas_call(_pair_sum_kernel, out_shape=jax.ShapeDtypeStruct(x.shape,...  40.6 us
    ppermute x1, waiting for transfers between devices, on_device(): theirs = lax.ppermute(mine, 'half', swap)  36.8 us
    ppermute x1, waiting for transfers between devices, on_device(): lax.ppermute(row_grad(other[3], other[4]).astype(jnp.bfloat16), 'half', s...  20.7 us
    all_gather x1, waiting for transfers between devices, on_device(): lax.all_gather(latent_up, 'dp', axis=0, tiled=True)  19.2 us
    all_gather x1, waiting for transfers between devices, on_device(): lax.all_gather(latent_down, 'dp', axis=1, tiled=True)  16.5 us
    dot_general x2, matrix products, forward(): jnp.einsum('necj,ehj->nech', rows_back, output_full, preferred_element_ty...  8.82 us
  transfers between devices with their start and end apart: 10, of which 4 were waited for; matrix products, arithmetic and copies ran while one was open for 24% of the time, Pallas kernels for 48%

profile of v3, /device:TPU:64, one launch (start us, length us, event | category | flops | bytes accessed | tf_op | source)
XLA Modules:
  0.0 417.4 jit_solution(17630807416197422425)
XLA Ops:
  7.2 0.7 all-gather.6.cloned.1.call-update
  8.0 0.7 all-gather.8.cloned.1.call-update
  8.7 0.7 all-gather.12.cloned.1.call-update
  11.7 2.6 gather_fusion.1
  14.6 16.5 %all-gather.6.cloned.1.call-done = bf16[2048,1024]{1,0:T(8,128)(2,1)} async-done(((bf16[2048,512]{1,0:T(8,128)(2,1)}), bf16[2048,1024]{1,0:T(8,128)(2,1)}) %all-gather.6.cloned.1.call-update) | async-done | bytes 4194320 | tf_op jit(solution)/shard_map/all_gather | solution.py:134
  31.1 2.9 fusion.73
  34.0 19.2 %all-gather.8.cloned.1.call-done = bf16[1024,2048]{1,0:T(8,128)(2,1)} async-done(((bf16[512,2048]{1,0:T(8,128)(2,1)}), bf16[1024,2048]{1,0:T(8,128)(2,1)}) %all-gather.8.cloned.1.call-update) | async-done | bytes 4194320 | tf_op jit(solution)/shard_map/all_gather | solution.py:135
  53.2 3.7 fusion.74
  56.9 1.1 pad_maximum_fusion.1.x_ref
  58.1 27.7 %shard_map.129 = f32[128,2048]{1,0:T(8,128)} custom-call(f32[128,2048]{1,0:T(8,128)} %pad_maximum_fusion.1.x_ref), custom_call_target="tpu_custom_call" | custom-call | tf_op jit(solution)/shard_map/pallas_call | solution.py:32
  85.8 1.2 slice.49
  87.1 2.5 gather_fusion.2
  89.6 2.2 gather.20
  91.8 2.9 gather_fusion
  95.4 1.9 copy-done.2
  97.8 2.8 pad_maximum_fusion.x_ref
  100.6 103.0 %shard_map.130 = bf16[64,9,2048]{2,1,0:T(8,128)(2,1)} custom-call(bf16[64,9,2048]{2,1,0:T(8,128)(2,1)} %pad_maximum_fusion.x_ref), custom_call_target="tpu_custom_call" | custom-call | tf_op jit(solution)/shard_map/pallas_call | solution.py:98
  203.7 3.6 copy.86
  208.5 4.2 slice_bitcast_fusion.1
  212.7 0.7 copy.83
  213.4 3.7 fusion.39
  217.2 2.6 fusion.33
  219.8 2.5 fusion.52
  222.3 36.8 %collective-permute-done = bf16[64,1,9,2048]{3,0,2,1:T(8,128)(2,1)} collective-permute-done((bf16[64,1,9,2048]{3,0,2,1:T(8,128)(2,1)S(1)}, bf16[64,1,9,2048]{3,0,2,1:T(8,128)(2,1)}, u32[]{:S(2)}, u32[]{:S(2)}) %collective-permute-start) | collective-permute-done | bytes 2359328 | tf_op jit(solution)/shard_map/ppermute | solution.py:171
  259.1 2.4 fusion.29
  261.5 3.0 fusion.36
  264.5 1.2 copy-done.23
  265.7 4.2 %fusion.47 = bf16[1,768,1024]{2,1,0:T(8,128)(2,1)} fusion(f32[768,1024,1]{1,0,2:T(8,128)S(1)} %fusion.52, bf16[64,1,9,2048]{3,0,2,1:T(8,128)(2,1)} %collective-permute-done, f32[64,9,768]{2,0,1:T(8,128)S(1)} %fusion.36, f32[64,9,768]{2,0,1:T(8,128)S(1)} %fusion.29), kind=kOutput, calls=%fused_computation.78 | convolution fusion | flops 910196736 | bytes 9437184 | tf_op jit(solution)/shard_map/nech,necj->ehj/dot_general | solution.py:208
  270.2 6.0 %fusion.22 = (bf16[64,1,9,768]{3,0,2,1:T(8,128)(2,1)S(1)}, bf16[64,1,9,768]{3,0,2,1:T(8,128)(2,1)}) fusion(f32[64,9,768]{2,0,1:T(8,128)} %copy-done.20, f32[64,9,768]{2,0,1:T(8,128)} %fusion.39, bf16[1,768,1024]{2,1,0:T(8,128)(2,1)} %all-gather.10.cloned.1.call-done, bf16[64,9,1024]{2,1,0:T(8,128)(2,1)S(1)} %copy-done.4), kind=kOutput, calls=%fused_computation.49 | convolution fusion | flops 911720448 | bytes 8060928 | tf_op jit(solution)/shard_map/necj,ehj->nech/dot_general | solution.py:182
  276.2 1.4 fusion.58
  279.0 2.9 fusion.16
  281.9 0.9 copy-done.15
  282.8 4.1 fusion.46
  286.9 1.4 fusion.61
  288.4 4.0 fusion.45
  292.7 2.9 fusion.27
  295.6 2.2 fusion.48
  297.8 0.8 collective-permute-start.1
  298.7 3.4 fusion.31
  302.1 1.1 convolution_add_fusion
  303.2 20.7 %collective-permute-done.1 = bf16[64,1,9,1024]{3,0,2,1:T(8,128)(2,1)S(1)} collective-permute-done((bf16[64,1,9,1024]{3,0,2,1:T(8,128)(2,1)}, bf16[64,1,9,1024]{3,0,2,1:T(8,128)(2,1)S(1)}, u32[]{:S(2)}, u32[]{:S(2)}) %collective-permute-start.1) | collective-permute-done | bytes 1179680 | tf_op jit(solution)/shard_map/ppermute | solution.py:215
  323.9 3.2 fusion.6.x_ref
  327.1 56.9 %shard_map.131 = bf16[64,9,1024]{2,1,0:T(8,128)(2,1)} custom-call(bf16[64,9,1024]{2,1,0:T(8,128)(2,1)} %fusion.6.x_ref), custom_call_target="tpu_custom_call" | custom-call | tf_op jit(solution)/shard_map/pallas_call | solution.py:98
  384.1 2.5 reshape_reshape.4
  386.6 4.1 gather_fusion.3
  390.7 2.1 fusion.x_ref
  392.8 12.9 %shard_map.132 = f32[128,1024]{1,0:T(8,128)} custom-call(f32[128,1024]{1,0:T(8,128)} %fusion.x_ref), custom_call_target="tpu_custom_call" | custom-call | tf_op jit(solution)/shard_map/pallas_call | solution.py:32
  405.7 4.7 %convolution_convert_fusion = bf16[128,2048]{1,0:T(8,128)(2,1)} fusion(bf16[2048,1024]{1,0:T(8,128)(2,1)} %all-gather.6.cloned.1.call-done, f32[128,1024]{1,0:T(8,128)} %shard_map.132), kind=kOutput, calls=%fused_computation.18 | convolution fusion | flops 537264128 | bytes 5242880 | tf_op jit(solution)/shard_map/dot_general | solution.py:238
  (91 shorter events, 7.1 us)
Async XLA Ops:
  7.2 23.9 %copy-start = (bf16[128,2048]{1,0:T(8,128)(2,1)S(1)}, bf16[128,2048]{1,0:T(8,128)(2,1)}, u32[]{:S(2)}) copy-start(bf16[128,2048]{1,0:T(8,128)(2,1)} %param.10) | copy-start | bytes 1572868
  7.2 23.9 %all-gather.6.cloned.1.call-start = ((), (), s32[]{:S(2)}) async-start(), calls=%async_computation.3 | async-start | bytes 6291456 | tf_op jit(solution)/shard_map/all_gather | solution.py:134
  7.9 2.2 copy-start.10
  7.9 2.2 copy-start.12
  7.9 3.5 copy-start.11
  7.9 45.3 %all-gather.8.cloned.1.call-start = ((), (), s32[]{:S(2)}) async-start(), calls=%async_computation.4 | async-start | bytes 6291456 | tf_op jit(solution)/shard_map/all_gather | solution.py:135
  8.7 204.7 %all-gather.12.cloned.1.call-start = ((), (), s32[]{:S(2)}) async-start(), calls=%async_computation.6 | async-start | bytes 2359296 | tf_op jit(solution)/shard_map/all_gather | solution.py:137
  9.4 207.7 %all-gather.14.cloned.1.call-start = ((), (), s32[]{:S(2)}) async-start(), calls=%async_computation.7 | async-start | bytes 2359296 | tf_op jit(solution)/shard_map/all_gather | solution.py:136
  10.0 260.2 %all-gather.10.cloned.1.call-start = ((), (), s32[]{:S(2)}) async-start(), calls=%async_computation.5 | async-start | bytes 2359296 | tf_op jit(solution)/shard_map/all_gather | solution.py:138
  14.6 38.7 %copy-start.9 = (bf16[128,2048]{1,0:T(8,128)(2,1)S(1)}, bf16[128,2048]{1,0:T(8,128)(2,1)}, u32[]{:S(2)}) copy-start(bf16[128,2048]{1,0:T(8,128)(2,1)} %param.11) | copy-start | bytes 1572868
  85.8 1.3 slice-start
  95.2 2.2 copy-start.2
  207.3 51.8 %collective-permute-start = (bf16[64,1,9,2048]{3,0,2,1:T(8,128)(2,1)S(1)}, bf16[64,1,9,2048]{3,0,2,1:T(8,128)(2,1)}, u32[]{:S(2)}, u32[]{:S(2)}) collective-permute-start(bf16[64,1,9,2048]{3,0,2,1:T(8,128)(2,1)S(1)} %copy.86), channel_id=1, source_target_pairs={{0,2},{2,0},{1,3},{3,1},{4,6},{6,4},{5,7},{7,5},{8,10},{10,8},{9,1... | collective-permute-start | bytes 7077896 | tf_op jit(solution)/shard_map/ppermute | solution.py:171
  208.0 202.4 %reduce-scatter.8.cloned.1.call-start = ((), (), s32[]{:S(2)}) async-start(), calls=%async_computation.10 | async-start | bytes 2359296 | tf_op jit(solution)/shard_map/reduce_scatter | solution.py:227
  217.1 2.7 copy-start.3
  217.2 2.7 copy-start.19
  219.8 2.5 copy-start.20
  219.8 39.3 %copy-start.13 = (bf16[1,1024,768]{2,1,0:T(8,128)(2,1)S(1)}, bf16[1,1024,768]{2,1,0:T(8,128)(2,1)}, u32[]{:S(2)}) copy-start(bf16[1,1024,768]{2,1,0:T(8,128)(2,1)} %all-gather.14.cloned.1.call-done) | copy-start | bytes 4718596
  222.3 39.1 %copy-start.5 = (bf16[1,1024,768]{2,1,0:T(8,128)(2,1)S(1)}, bf16[1,1024,768]{2,1,0:T(8,128)(2,1)}, u32[]{:S(2)}) copy-start(bf16[1,1024,768]{2,1,0:T(8,128)(2,1)} %all-gather.12.cloned.1.call-done) | copy-start | bytes 4718596
  261.5 3.0 copy-start.21
  264.5 1.2 copy-start.23
  265.7 4.5 %copy-start.4 = (bf16[64,9,1024]{2,1,0:T(8,128)(2,1)S(1)}, bf16[64,9,1024]{2,1,0:T(8,128)(2,1)}, u32[]{:S(2)}) copy-start(bf16[64,9,1024]{2,1,0:T(8,128)(2,1)} %get-tuple-element.6) | copy-start | bytes 3538948
  269.9 140.4 %reduce-scatter.6.cloned.1.call-start = ((), (), s32[]{:S(2)}) async-start(), calls=%async_computation.9 | async-start | bytes 2359296 | tf_op jit(solution)/shard_map/reduce_scatter | solution.py:224
  276.2 1.5 copy-start.7
  276.2 1.7 copy-start.14
  276.2 2.3 copy-start.22
  276.2 2.8 copy-start.24
  281.8 0.9 copy-start.15
  281.8 6.5 %copy-start.18 = (bf16[64,1,9,768]{3,0,2,1:T(8,128)(2,1)}, bf16[64,1,9,768]{3,0,2,1:T(8,128)(2,1)S(1)}, u32[]{:S(2)}) copy-start(bf16[64,1,9,768]{3,0,2,1:T(8,128)(2,1)S(1)} %get-tuple-element.9) | copy-start | bytes 2654212
  282.8 4.1 copy-start.17
  286.9 123.5 %reduce-scatter.4.cloned.1.call-start = ((), (), s32[]{:S(2)}) async-start(), calls=%async_computation.8 | async-start | bytes 2359296 | tf_op jit(solution)/shard_map/reduce_scatter | solution.py:221
  292.6 3.0 copy-start.6
  292.6 3.0 copy-start.16
  297.8 26.1 %collective-permute-start.1 = (bf16[64,1,9,1024]{3,0,2,1:T(8,128)(2,1)}, bf16[64,1,9,1024]{3,0,2,1:T(8,128)(2,1)S(1)}, u32[]{:S(2)}, u32[]{:S(2)}) collective-permute-start(bf16[64,1,9,1024]{3,0,2,1:T(8,128)(2,1)} %fusion.48), channel_id=1, source_target_pairs={{0,2},{2,0},{1,3},{3,1},{4,6},{6,4},{5,7},{7,5},{8,10},{10,8},{9,1... | collective-permute-start | bytes 3538952 | tf_op jit(solution)/shard_map/ppermute | solution.py:215
  298.7 3.4 copy-start.8
  392.8 17.5 %copy-start.1 = (bf16[128,2048]{1,0:T(8,128)(2,1)S(1)}, bf16[128,2048]{1,0:T(8,128)(2,1)}, u32[]{:S(2)}) copy-start(bf16[128,2048]{1,0:T(8,128)(2,1)} %param.10) | copy-start | bytes 1572868
Sparse Core Ops, SparseCore 0:
  9.8 21.2 all-gather.5
  32.9 20.2 all-gather.7
  55.0 16.4 all-gather.11
  73.1 16.4 all-gather.13
  208.1 15.6 all-gather.9
  270.1 13.9 reduce-scatter.7
  287.3 15.7 reduce-scatter.5
  306.1 15.7 reduce-scatter.3
